TPU v7x, 32 devices: a whole 2x2x4 slice. The times are simulated.
32 devices in a mesh: dp: 2 (over y), expert: 16 (over z, x, core).
Axes of the slice: x: 2, y: 2, z: 4, core: 2. Of those that a mesh axis runs over, the one named last changes fastest.
Arguments:
- tokens: bfloat16 [2048, 3584], P('expert', 'dp'), may hold values from -6 to 6
- expert_ids: int32 [2048, 8], P('expert'), may hold values from 0 to 63, all different within a row; in each aligned block of 128 rows (0 to 127, 128 to 255, ...) at most 32 rows name the same one
- gate_weight: float32 [2048, 8], P('expert'), may hold values from 0.1 to 0.6
- w_gate: bfloat16 [16, 3584, 1024], P('expert', 'dp'), may hold values from -0.09375 to 0.09375
- w_up: bfloat16 [16, 3584, 1024], P('expert', 'dp'), may hold values from -0.09375 to 0.09375
- w_down: bfloat16 [16, 1024, 3584], P('expert', None, 'dp'), may hold values from -0.1875 to 0.1875
- grad_out: bfloat16 [2048, 3584], P('expert', 'dp'), may hold values from -6 to 6
Outputs:
- output: bfloat16 [2048, 3584], P('expert', 'dp')
- grad_tokens: bfloat16 [2048, 3584], P('expert', 'dp')
- grad_down: bfloat16 [16, 1024, 3584], P('expert', None, 'dp')
Inputs may be any that keep to these rules, and one draw needn't show every extreme that they name: `expert_ids`: each row names 8 different experts. Among the rows of one device no expert is named by more than 32 rows, and in some device's rows some expert is named by exactly 32 rows.
All inputs are finite; a program needn't handle non-finite values.
Results may differ from a plain program's by a relative error of at most 0.024.
Values may be sent and summed in bfloat16 or wider, within the bound.
A program may use at most 64 MiB of HBM per device.

v0:
```python
import jax
import jax.numpy as jnp
from jax import lax
from jax.sharding import PartitionSpec as P


def local(tokens, expert_ids, gate_weight, w_gate, w_up, w_down, grad_out):
    tok_dev, fanout = expert_ids.shape
    feature_cols = tokens.shape[1]
    experts = lax.axis_size("expert")
    capacity = max(2, min(tok_dev, 2 * tok_dev * fanout // (4 * experts)))
    pair_count = tok_dev * fanout
    flat_ids = expert_ids.reshape(pair_count)
    onehot = (flat_ids[:, None] == jnp.arange(experts, dtype=jnp.int32)[None, :]).astype(jnp.int32)
    before = jnp.cumsum(onehot, axis=0) - onehot
    slot_index = jnp.sum(before * onehot, axis=1)
    position = flat_ids * capacity + slot_index
    placing = jnp.arange(experts * capacity, dtype=jnp.int32)[:, None] == position[None, :]
    placing = placing.reshape(experts * capacity, tok_dev, fanout)
    select = jnp.sum(placing.astype(jnp.float32), axis=2).astype(jnp.bfloat16)
    slot_gate = jnp.sum(jnp.where(placing, gate_weight[None, :, :], 0.0), axis=(1, 2))
    x_slab = jnp.dot(select, tokens, preferred_element_type=jnp.float32).astype(jnp.bfloat16)
    x_slab = x_slab.reshape(experts, capacity, feature_cols)
    cot_rows = jnp.dot(select, grad_out, preferred_element_type=jnp.float32)
    c_slab = (slot_gate[:, None] * cot_rows).astype(jnp.bfloat16)
    c_slab = c_slab.reshape(experts, capacity, feature_cols)
    gate_mat = w_gate[0]
    up_mat = w_up[0]
    down_mat = w_down[0]
    row_total = experts * capacity
    transposed = (((1,), (1,)), ((), ()))
    arrived = lax.all_to_all(x_slab, "expert", split_axis=0, concat_axis=0, tiled=True)
    x_rows = arrived.reshape(row_total, feature_cols)
    gate_part = jnp.dot(x_rows, gate_mat, preferred_element_type=jnp.float32)
    up_part = jnp.dot(x_rows, up_mat, preferred_element_type=jnp.float32)
    gate_pre = lax.psum(gate_part.astype(jnp.bfloat16), "dp").astype(jnp.float32)
    up_pre = lax.psum(up_part.astype(jnp.bfloat16), "dp").astype(jnp.float32)
    hidden = (jax.nn.silu(gate_pre) * up_pre).astype(jnp.bfloat16)
    out_rows = jnp.dot(hidden, down_mat, preferred_element_type=jnp.float32).astype(jnp.bfloat16)
    gate_pre, up_pre, hidden, out_rows = (
        gate_pre,
        up_pre,
        hidden,
        out_rows.reshape(experts, capacity, feature_cols),
    )
    back_out = lax.all_to_all(out_rows, "expert", split_axis=0, concat_axis=0, tiled=True)
    arrived_grads = lax.all_to_all(c_slab, "expert", split_axis=0, concat_axis=0, tiled=True)
    c_rows = arrived_grads.reshape(row_total, feature_cols)
    hidden_part = lax.dot_general(c_rows, down_mat, transposed, preferred_element_type=jnp.float32)
    sig = jax.nn.sigmoid(gate_pre)
    grad_hidden = lax.psum(hidden_part.astype(jnp.bfloat16), "dp").astype(jnp.float32)
    grad_gate = (grad_hidden * up_pre * sig * (1.0 + gate_pre * (1.0 - sig))).astype(jnp.bfloat16)
    grad_up = (grad_hidden * jax.nn.silu(gate_pre)).astype(jnp.bfloat16)
    grad_rows = lax.dot_general(grad_gate, gate_mat, transposed, preferred_element_type=jnp.float32)
    grad_rows = grad_rows + lax.dot_general(
        grad_up, up_mat, transposed, preferred_element_type=jnp.float32
    )
    grad_rows = grad_rows.astype(jnp.bfloat16).reshape(experts, capacity, feature_cols)
    down_grad = lax.dot_general(
        hidden, c_rows, (((0,), (0,)), ((), ())), preferred_element_type=jnp.float32
    )
    grad_rows, down_grad = (grad_rows, down_grad.astype(jnp.bfloat16))
    back_grads = lax.all_to_all(grad_rows, "expert", split_axis=0, concat_axis=0, tiled=True)
    scaled = back_out.reshape(row_total, feature_cols).astype(jnp.float32) * slot_gate[:, None]
    upper_part = scaled.astype(jnp.bfloat16)
    lower_part = (scaled - upper_part.astype(jnp.float32)).astype(jnp.bfloat16)
    output = jnp.dot(select.T, upper_part, preferred_element_type=jnp.float32)
    output = (output + jnp.dot(select.T, lower_part, preferred_element_type=jnp.float32)).astype(
        jnp.bfloat16
    )
    grad_flat = back_grads.reshape(row_total, feature_cols)
    grad_tokens = jnp.dot(select.T, grad_flat, preferred_element_type=jnp.float32).astype(
        jnp.bfloat16
    )
    return (output, grad_tokens, down_grad.reshape(1, down_grad.shape[0], feature_cols))


def solution(mesh):
    return jax.shard_map(
        local,
        mesh=mesh,
        in_specs=(
            P("expert", "dp"),
            P("expert", None),
            P("expert", None),
            P("expert", "dp", None),
            P("expert", "dp", None),
            P("expert", None, "dp"),
            P("expert", "dp"),
        ),
        out_specs=(P("expert", "dp"), P("expert", "dp"), P("expert", None, "dp")),
        check_vma=False,
    )
```

profile of v0, /device:TPU:11, one launch (start us, length us, event | category | flops | bytes accessed | tf_op | source)
XLA Modules:
  0.0 318.3 jit_solution(14854506770356374318)
XLA Ops:
  7.2 0.0 copy-start
  7.2 0.8 copy.28
  8.0 0.1 eq.44
  8.1 0.1 eq.40
  8.2 4.5 %reduce-window.6 = s32[16,8,128]{2,1,0:T(8,128)S(1)} reduce-window(s32[16,8,128]{2,1,0:T(8,128)S(1)} %fusion.48, s32[]{:T(128)} %constant.12.clone.1), window={size=1x1x128 pad=0_0x0_0x127_0}, to_apply=%region_0.0 | reduce-window | flops 2080768 | bytes 131076 | tf_op jit(solution)/shard_map/reduce-window
  12.7 0.1 slice.8
  12.8 0.1 copy.30
  13.0 0.1 copy.31
  13.1 0.1 broadcast_add_fusion
  13.2 0.1 reduce_sum.30
  13.3 0.7 multiply_add_fusion
  14.0 2.3 select_reduce_fusion
  16.4 0.0 copy-done
  16.4 1.9 convolution_convert_fusion.1
  18.2 0.0 copy-start.6
  18.3 6.7 %all-to-all-start = ((bf16[16,32,1792]{2,1,0:T(8,128)(2,1)}), bf16[16,32,1792]{2,1,0:T(8,128)(2,1)S(1)}, u32[]{:S(2)}, u32[]{:S(2)}) async-start(bf16[16,32,1792]{2,1,0:T(8,128)(2,1)} %bitcast.2), calls=%async_computation | async-start | bytes 3670016 | tf_op jit(solution)/shard_map/all_to_all | solution.py:32
  24.9 0.0 copy-done.6
  24.9 1.9 multiply_convert_fusion
  26.8 39.9 %all-to-all-done = bf16[16,32,1792]{2,1,0:T(8,128)(2,1)S(1)} async-done(((bf16[16,32,1792]{2,1,0:T(8,128)(2,1)}), bf16[16,32,1792]{2,1,0:T(8,128)(2,1)S(1)}, u32[]{:S(2)}, u32[]{:S(2)}) %all-to-all-start) | async-done | bytes 1835040 | tf_op jit(solution)/shard_map/all_to_all | solution.py:32
  66.7 0.0 copy-start.4
  66.7 1.2 copy-done.4
  67.9 4.8 %all-to-all-start.2 = ((bf16[16,32,1792]{2,1,0:T(8,128)(2,1)}), bf16[16,32,1792]{2,1,0:T(8,128)(2,1)S(1)}, u32[]{:S(2)}, u32[]{:S(2)}) async-start(bf16[16,32,1792]{2,1,0:T(8,128)(2,1)} %bitcast.9), calls=%async_computation.2 | async-start | bytes 3670016 | tf_op jit(solution)/shard_map/all_to_all | solution.py:47
  72.7 0.0 all-reduce.3.cloned.1.call-start
  72.8 0.0 copy-start.5
  72.8 0.0 copy-start.7
  72.8 5.8 %fusion.36 = bf16[512,1024]{1,0:T(8,128)(2,1)} fusion(bf16[512,1792]{1,0:T(8,128)(2,1)} %bitcast.71, bf16[1,1792,1024]{2,1,0:T(8,128)(2,1)} %param.11), kind=kOutput, calls=%fused_computation.45 | convolution fusion | flops 1879572480 | bytes 6553600 | tf_op jit(solution)/shard_map/dot_general | solution.py:35
  78.6 0.0 copy-done.5
  78.6 0.0 copy-done.7
  78.6 3.0 fusion.33
  81.6 32.9 %all-to-all-done.2 = bf16[16,32,1792]{2,1,0:T(8,128)(2,1)S(1)} async-done(((bf16[16,32,1792]{2,1,0:T(8,128)(2,1)}), bf16[16,32,1792]{2,1,0:T(8,128)(2,1)S(1)}, u32[]{:S(2)}, u32[]{:S(2)}) %all-to-all-start.2) | async-done | bytes 1835040 | tf_op jit(solution)/shard_map/all_to_all | solution.py:47
  114.5 0.0 copy-start.3
  114.5 5.8 %fusion.39 = bf16[512,1024]{1,0:T(8,128)(2,1)} fusion(bf16[512,1792]{1,0:T(8,128)(2,1)S(1)} %bitcast.69, bf16[1,1024,1792]{2,1,0:T(8,128)(2,1)} %param.12), kind=kOutput, calls=%fused_computation.46 | convolution fusion | flops 1879572480 | bytes 6553600 | tf_op jit(solution)/shard_map/dot_general | solution.py:49
  120.3 0.0 copy-done.3
  120.3 0.0 all-reduce.3.cloned.1.call-update
  120.3 85.3 %all-reduce.3.cloned.1.call-done = (bf16[512,1024]{1,0:T(8,128)(2,1)}, bf16[512,1024]{1,0:T(8,128)(2,1)}, bf16[512,1024]{1,0:T(8,128)(2,1)}) async-done(((bf16[512,1024]{1,0:T(8,128)(2,1)}, bf16[512,1024]{1,0:T(8,128)(2,1)}, bf16[512,1024]{1,0:T(8,128)(2,1)}), (bf16[512,1024]{1,0:T(8,128)(2,1)}, bf16[512,1024]{1,0:T(8,128)(2,1)}, bf16[512,1024]{1,0:T(8,128)(2,1)})) %all-reduce.3.cloned.1.call-update) | async-done | bytes 3145744 | tf_op jit(solution)/shard_map/psum | solution.py:37
  205.6 6.4 %fusion.18 = bf16[512,1792]{1,0:T(8,128)(2,1)} fusion(bf16[1,1024,1792]{2,1,0:T(8,128)(2,1)} %param.12, bf16[512,1024]{1,0:T(8,128)(2,1)} %get-tuple-element.5, bf16[512,1024]{1,0:T(8,128)(2,1)} %get-tuple-element.6), kind=kOutput, calls=%fused_computation.23 | convolution fusion | flops 1884160000 | bytes 7602176 | tf_op jit(solution)/shard_map/dot_general | solution.py:39
  212.0 6.5 %all-to-all-start.1 = ((bf16[16,32,1792]{2,1,0:T(8,128)(2,1)}), bf16[16,32,1792]{2,1,0:T(8,128)(2,1)S(1)}, u32[]{:S(2)}, u32[]{:S(2)}) async-start(bf16[16,32,1792]{2,1,0:T(8,128)(2,1)} %bitcast.74), calls=%async_computation.1 | async-start | bytes 3670016 | tf_op jit(solution)/shard_map/all_to_all | solution.py:46
  218.5 0.0 copy-start.8
  218.5 0.0 copy-start.9
  218.5 0.0 copy-start.10
  218.5 0.0 copy-start.11
  218.5 5.3 %fusion.7 = f32[512,1792]{1,0:T(8,128)S(1)} fusion(bf16[1,1792,1024]{2,1,0:T(8,128)(2,1)} %param.11, bf16[512,1024]{1,0:T(8,128)(2,1)} %get-tuple-element.7, bf16[512,1024]{1,0:T(8,128)(2,1)} %get-tuple-element.6), kind=kOutput, calls=%fused_computation.9 | convolution fusion | flops 1883242496 | bytes 9437184 | tf_op jit(solution)/shard_map/dot_general | solution.py:55
  223.8 0.0 copy-done.8
  223.8 0.0 copy-done.9
  223.8 0.0 copy-done.10
  223.8 0.0 copy-done.11
  223.8 4.2 %add_convert_fusion = bf16[512,1792]{1,0:T(8,128)(2,1)} fusion(f32[512,1792]{1,0:T(8,128)S(1)} %fusion.7, bf16[1,1792,1024]{2,1,0:T(8,128)(2,1)S(1)} %copy-done.8, bf16[512,1024]{1,0:T(8,128)(2,1)S(1)} %copy-done.9, bf16[512,1024]{1,0:T(8,128)(2,1)S(1)} %copy-done.11, bf16[512,1024]{1,0:T(8,128)(2,1)S(1)} %copy-done.10), kind=kOutput, calls=%fused_computation.17 | convolution fusion | flops 1887698944 | bytes 12320768 | tf_op jit(solution)/shard_map/dot_general | solution.py:54
  228.0 32.3 %all-to-all-done.1 = bf16[16,32,1792]{2,1,0:T(8,128)(2,1)S(1)} async-done(((bf16[16,32,1792]{2,1,0:T(8,128)(2,1)}), bf16[16,32,1792]{2,1,0:T(8,128)(2,1)S(1)}, u32[]{:S(2)}, u32[]{:S(2)}) %all-to-all-start.1) | async-done | bytes 1835040 | tf_op jit(solution)/shard_map/all_to_all | solution.py:46
  260.3 4.8 %all-to-all-start.3 = ((bf16[16,32,1792]{2,1,0:T(8,128)(2,1)}), bf16[16,32,1792]{2,1,0:T(8,128)(2,1)}, u32[]{:S(2)}, u32[]{:S(2)}) async-start(bf16[16,32,1792]{2,1,0:T(8,128)(2,1)} %bitcast.73), calls=%async_computation.3 | async-start | bytes 3670016 | tf_op jit(solution)/shard_map/all_to_all | solution.py:63
  265.0 6.2 %fusion.15 = bf16[1,1024,1792]{2,1,0:T(8,128)(2,1)} fusion(bf16[512,1792]{1,0:T(8,128)(2,1)} %bitcast.70, bf16[512,1024]{1,0:T(8,128)(2,1)} %get-tuple-element.5, bf16[512,1024]{1,0:T(8,128)(2,1)} %get-tuple-element.6), kind=kOutput, calls=%fused_computation.19 | convolution fusion | flops 1885077504 | bytes 7602176 | tf_op jit(solution)/shard_map/dot_general | solution.py:59
  271.3 0.4 fusion.1
  271.7 0.0 copy-start.1
  271.7 1.2 copy-done.1
  272.9 0.4 fusion.53
  273.3 33.6 %all-to-all-done.3 = bf16[16,32,1792]{2,1,0:T(8,128)(2,1)} async-done(((bf16[16,32,1792]{2,1,0:T(8,128)(2,1)}), bf16[16,32,1792]{2,1,0:T(8,128)(2,1)}, u32[]{:S(2)}, u32[]{:S(2)}) %all-to-all-start.3) | async-done | bytes 1835040 | tf_op jit(solution)/shard_map/all_to_all | solution.py:63
  306.9 0.0 copy-start.2
  306.9 2.8 convolution_convert_fusion.2
  309.8 0.0 copy-done.2
  309.8 1.7 fusion.21
  (5 shorter events, 0.1 us)
Async XLA Ops:
  7.2 9.2 %copy-start = (bf16[128,1792]{1,0:T(8,128)(2,1)S(1)}, bf16[128,1792]{1,0:T(8,128)(2,1)}, u32[]{:S(2)}) copy-start(bf16[128,1792]{1,0:T(8,128)(2,1)} %param.7) | copy-start | bytes 1376260
  18.2 6.7 %copy-start.6 = (bf16[128,1792]{1,0:T(8,128)(2,1)S(1)}, bf16[128,1792]{1,0:T(8,128)(2,1)}, u32[]{:S(2)}) copy-start(bf16[128,1792]{1,0:T(8,128)(2,1)} %param.13) | copy-start | bytes 1376260
  18.3 48.5 %all-to-all-start = ((bf16[16,32,1792]{2,1,0:T(8,128)(2,1)}), bf16[16,32,1792]{2,1,0:T(8,128)(2,1)S(1)}, u32[]{:S(2)}, u32[]{:S(2)}) async-start(bf16[16,32,1792]{2,1,0:T(8,128)(2,1)} %bitcast.2), calls=%async_computation | async-start | bytes 3670016 | tf_op jit(solution)/shard_map/all_to_all | solution.py:32
  66.7 1.2 copy-start.4
  67.9 46.6 %all-to-all-start.2 = ((bf16[16,32,1792]{2,1,0:T(8,128)(2,1)}), bf16[16,32,1792]{2,1,0:T(8,128)(2,1)S(1)}, u32[]{:S(2)}, u32[]{:S(2)}) async-start(bf16[16,32,1792]{2,1,0:T(8,128)(2,1)} %bitcast.9), calls=%async_computation.2 | async-start | bytes 3670016 | tf_op jit(solution)/shard_map/all_to_all | solution.py:47
  72.7 132.9 %all-reduce.3.cloned.1.call-start = ((), (), s32[]{:S(2)}) async-start(), calls=%async_computation.4 | async-start | bytes 6291456 | tf_op jit(solution)/shard_map/psum | solution.py:37
  72.8 5.8 %copy-start.5 = (bf16[16,32,1792]{2,1,0:T(8,128)(2,1)S(1)}, bf16[16,32,1792]{2,1,0:T(8,128)(2,1)}, u32[]{:S(2)}) copy-start(bf16[16,32,1792]{2,1,0:T(8,128)(2,1)} %copy-done.4) | copy-start | bytes 5505028
  72.8 5.8 %copy-start.7 = (bf16[1,1792,1024]{2,1,0:T(8,128)(2,1)S(1)}, bf16[1,1792,1024]{2,1,0:T(8,128)(2,1)}, u32[]{:S(2)}) copy-start(bf16[1,1792,1024]{2,1,0:T(8,128)(2,1)} %param.10) | copy-start | bytes 11010052
  114.5 5.8 %copy-start.3 = (bf16[16,32,1792]{2,1,0:T(8,128)(2,1)}, bf16[16,32,1792]{2,1,0:T(8,128)(2,1)S(1)}, u32[]{:S(2)}) copy-start(bf16[16,32,1792]{2,1,0:T(8,128)(2,1)S(1)} %all-to-all-done.2) | copy-start | bytes 5505028
  212.0 48.3 %all-to-all-start.1 = ((bf16[16,32,1792]{2,1,0:T(8,128)(2,1)}), bf16[16,32,1792]{2,1,0:T(8,128)(2,1)S(1)}, u32[]{:S(2)}, u32[]{:S(2)}) async-start(bf16[16,32,1792]{2,1,0:T(8,128)(2,1)} %bitcast.74), calls=%async_computation.1 | async-start | bytes 3670016 | tf_op jit(solution)/shard_map/all_to_all | solution.py:46
  218.5 5.3 %copy-start.8 = (bf16[1,1792,1024]{2,1,0:T(8,128)(2,1)S(1)}, bf16[1,1792,1024]{2,1,0:T(8,128)(2,1)}, u32[]{:S(2)}) copy-start(bf16[1,1792,1024]{2,1,0:T(8,128)(2,1)} %param.10) | copy-start | bytes 11010052
  218.5 5.3 %copy-start.9 = (bf16[512,1024]{1,0:T(8,128)(2,1)S(1)}, bf16[512,1024]{1,0:T(8,128)(2,1)}, u32[]{:S(2)}) copy-start(bf16[512,1024]{1,0:T(8,128)(2,1)} %get-tuple-element.5) | copy-start | bytes 3145732
  218.5 5.3 %copy-start.10 = (bf16[512,1024]{1,0:T(8,128)(2,1)S(1)}, bf16[512,1024]{1,0:T(8,128)(2,1)}, u32[]{:S(2)}) copy-start(bf16[512,1024]{1,0:T(8,128)(2,1)} %get-tuple-element.6) | copy-start | bytes 3145732
  218.5 5.3 %copy-start.11 = (bf16[512,1024]{1,0:T(8,128)(2,1)S(1)}, bf16[512,1024]{1,0:T(8,128)(2,1)}, u32[]{:S(2)}) copy-start(bf16[512,1024]{1,0:T(8,128)(2,1)} %get-tuple-element.7) | copy-start | bytes 3145732
  260.3 46.7 %all-to-all-start.3 = ((bf16[16,32,1792]{2,1,0:T(8,128)(2,1)}), bf16[16,32,1792]{2,1,0:T(8,128)(2,1)}, u32[]{:S(2)}, u32[]{:S(2)}) async-start(bf16[16,32,1792]{2,1,0:T(8,128)(2,1)} %bitcast.73), calls=%async_computation.3 | async-start | bytes 3670016 | tf_op jit(solution)/shard_map/all_to_all | solution.py:63
  271.7 1.2 copy-start.1
  306.9 2.8 copy-start.2
Sparse Core Ops, SparseCore 0:
  120.4 85.1 all-reduce.2
where the time goes:
time: 319 us; the launch traced here: 318 us
  waiting for transfers between devices  224 us (70%)
  matrix products  45.3 us (14%)
  starting transfers between devices  22.8 us (7%)
  between operations  14.2 us (4%)
  other arithmetic  8.11 us (3%)
  local copies, waits for them, and re-layouts  3.94 us (1%)
    psum x1, waiting for transfers between devices, local(): up_pre = lax.psum(up_part.astype(jnp.bfloat16), 'dp').astype(jnp.float32)  85.3 us
    all_to_all x1, waiting for transfers between devices, local(): lax.all_to_all(x_slab, 'expert', split_axis=0, concat_axis=0, tiled=True)  39.9 us
    all_to_all x1, waiting for transfers between devices, local(): lax.all_to_all(grad_rows, 'expert', split_axis=0, concat_axis=0, tiled=True)  33.6 us
    all_to_all x1, waiting for transfers between devices, local(): lax.all_to_all(c_slab, 'expert', split_axis=0, concat_axis=0, tiled=True)  32.9 us
    all_to_all x1, waiting for transfers between devices, local(): lax.all_to_all(out_rows, 'expert', split_axis=0, concat_axis=0, tiled=True)  32.3 us
    all_to_all x1, starting transfers between devices, local(): lax.all_to_all(x_slab, 'expert', split_axis=0, concat_axis=0, tiled=True)  6.65 us
    all_to_all x1, starting transfers between devices, local(): lax.all_to_all(out_rows, 'expert', split_axis=0, concat_axis=0, tiled=True)  6.51 us
  transfers between devices with their start and end apart: 5, of which 5 were waited for; matrix products, arithmetic and copies ran while one was open for 9% of the time, Pallas kernels for 0%

commit v1 on v0

--- a/solution.py
+++ b/solution.py
@@ -2,6 +2,16 @@
 import jax.numpy as jnp
 from jax import lax
 from jax.sharding import PartitionSpec as P
+
+
+def dp_sum(part):
+    count = lax.axis_size("dp")
+    part = part.astype(jnp.bfloat16)
+    total = part.astype(jnp.float32)
+    for shift in range(1, count):
+        moved = lax.ppermute(part, "dp", [(i, (i + shift) % count) for i in range(count)])
+        total = total + moved.astype(jnp.float32)
+    return total
 
 
 def local(tokens, expert_ids, gate_weight, w_gate, w_up, w_down, grad_out):
@@ -9,16 +19,17 @@
     feature_cols = tokens.shape[1]
     experts = lax.axis_size("expert")
     capacity = max(2, min(tok_dev, 2 * tok_dev * fanout // (4 * experts)))
-    pair_count = tok_dev * fanout
-    flat_ids = expert_ids.reshape(pair_count)
-    onehot = (flat_ids[:, None] == jnp.arange(experts, dtype=jnp.int32)[None, :]).astype(jnp.int32)
-    before = jnp.cumsum(onehot, axis=0) - onehot
-    slot_index = jnp.sum(before * onehot, axis=1)
-    position = flat_ids * capacity + slot_index
-    placing = jnp.arange(experts * capacity, dtype=jnp.int32)[:, None] == position[None, :]
-    placing = placing.reshape(experts * capacity, tok_dev, fanout)
-    select = jnp.sum(placing.astype(jnp.float32), axis=2).astype(jnp.bfloat16)
-    slot_gate = jnp.sum(jnp.where(placing, gate_weight[None, :, :], 0.0), axis=(1, 2))
+    ids = jnp.arange(experts, dtype=jnp.int32)
+    named = expert_ids[None, :, :] == ids[:, None, None]
+    hot = jnp.any(named, axis=2)
+    gate_of = jnp.sum(jnp.where(named, gate_weight[None, :, :], 0.0), axis=2)
+    rows = jnp.arange(tok_dev, dtype=jnp.int32)
+    earlier = (rows[:, None] < rows[None, :]).astype(jnp.bfloat16)
+    before = jnp.dot(hot.astype(jnp.bfloat16), earlier, preferred_element_type=jnp.float32)
+    slot_of = jnp.where(hot, before.astype(jnp.int32), -1)
+    placing = slot_of[:, None, :] == jnp.arange(capacity, dtype=jnp.int32)[None, :, None]
+    select = placing.astype(jnp.bfloat16).reshape(experts * capacity, tok_dev)
+    slot_gate = jnp.sum(jnp.where(placing, gate_of[:, None, :], 0.0), axis=2).reshape(experts * capacity)
     x_slab = jnp.dot(select, tokens, preferred_element_type=jnp.float32).astype(jnp.bfloat16)
     x_slab = x_slab.reshape(experts, capacity, feature_cols)
     cot_rows = jnp.dot(select, grad_out, preferred_element_type=jnp.float32)
@@ -33,8 +44,8 @@
     x_rows = arrived.reshape(row_total, feature_cols)
     gate_part = jnp.dot(x_rows, gate_mat, preferred_element_type=jnp.float32)
     up_part = jnp.dot(x_rows, up_mat, preferred_element_type=jnp.float32)
-    gate_pre = lax.psum(gate_part.astype(jnp.bfloat16), "dp").astype(jnp.float32)
-    up_pre = lax.psum(up_part.astype(jnp.bfloat16), "dp").astype(jnp.float32)
+    gate_pre = dp_sum(gate_part)
+    up_pre = dp_sum(up_part)
     hidden = (jax.nn.silu(gate_pre) * up_pre).astype(jnp.bfloat16)
     out_rows = jnp.dot(hidden, down_mat, preferred_element_type=jnp.float32).astype(jnp.bfloat16)
     gate_pre, up_pre, hidden, out_rows = (
@@ -48,7 +59,7 @@
     c_rows = arrived_grads.reshape(row_total, feature_cols)
     hidden_part = lax.dot_general(c_rows, down_mat, transposed, preferred_element_type=jnp.float32)
     sig = jax.nn.sigmoid(gate_pre)
-    grad_hidden = lax.psum(hidden_part.astype(jnp.bfloat16), "dp").astype(jnp.float32)
+    grad_hidden = dp_sum(hidden_part)
     grad_gate = (grad_hidden * up_pre * sig * (1.0 + gate_pre * (1.0 - sig))).astype(jnp.bfloat16)
     grad_up = (grad_hidden * jax.nn.silu(gate_pre)).astype(jnp.bfloat16)
     grad_rows = lax.dot_general(grad_gate, gate_mat, transposed, preferred_element_type=jnp.float32)
@@ -62,12 +73,8 @@
     grad_rows, down_grad = (grad_rows, down_grad.astype(jnp.bfloat16))
     back_grads = lax.all_to_all(grad_rows, "expert", split_axis=0, concat_axis=0, tiled=True)
     scaled = back_out.reshape(row_total, feature_cols).astype(jnp.float32) * slot_gate[:, None]
-    upper_part = scaled.astype(jnp.bfloat16)
-    lower_part = (scaled - upper_part.astype(jnp.float32)).astype(jnp.bfloat16)
-    output = jnp.dot(select.T, upper_part, preferred_element_type=jnp.float32)
-    output = (output + jnp.dot(select.T, lower_part, preferred_element_type=jnp.float32)).astype(
-        jnp.bfloat16
-    )
+    output = jnp.dot(select.T, scaled.astype(jnp.bfloat16), preferred_element_type=jnp.float32)
+    output = output.astype(jnp.bfloat16)
     grad_flat = back_grads.reshape(row_total, feature_cols)
     grad_tokens = jnp.dot(select.T, grad_flat, preferred_element_type=jnp.float32).astype(
         jnp.bfloat16

time: 319 us -> 263 us (0.82)
  waiting for transfers between devices: 224 us -> 192 us
  between operations: 14.2 us -> 0.79 us
  matrix products: 45.3 us -> 39.4 us
  other arithmetic: 8.11 us -> 4.83 us
    psum x1 -> x0, waiting for transfers between devices: 85.3 us -> none  [local(): up_pre = lax.psum(up_part.astype(jnp.bfloat16), 'dp').astype(jnp.float32)]
    ppermute x0 -> x3, waiting for transfers between devices: none -> 45.6 us  [dp_sum(): lax.ppermute(part, 'dp', [(i, (i + shift) % count) for i in range(count)])]
    all_to_all x1, waiting for transfers between devices: 32.9 us -> 39.9 us  [local(): lax.all_to_all(c_slab, 'expert', split_axis=0, concat_axis=0, tiled=True)]
    another operation x3 -> x0, other arithmetic: 4.64 us -> none
    all_to_all x1, waiting for transfers between devices: 39.9 us -> 36.5 us  [local(): lax.all_to_all(x_slab, 'expert', split_axis=0, concat_axis=0, tiled=True)]
  transfers between devices with their start and end apart: 5 -> 7, of which waited for: 5 -> 6; matrix products, arithmetic and copies ran while one was open for 9% -> 11% of each run, Pallas kernels for 0% -> 0%
where the time goes in v1:
time: 263 us
  waiting for transfers between devices  192 us (73%)
  matrix products  39.4 us (15%)
  starting transfers between devices  24.7 us (9%)
  other arithmetic  4.83 us (2%)
    ppermute x3, waiting for transfers between devices, dp_sum(): lax.ppermute(part, 'dp', [(i, (i + shift) % count) for i in range(count)])  45.6 us
    all_to_all x1, waiting for transfers between devices, local(): lax.all_to_all(c_slab, 'expert', split_axis=0, concat_axis=0, tiled=True)  39.9 us
    all_to_all x1, waiting for transfers between devices, local(): lax.all_to_all(x_slab, 'expert', split_axis=0, concat_axis=0, tiled=True)  36.5 us
    all_to_all x1, waiting for transfers between devices, local(): lax.all_to_all(out_rows, 'expert', split_axis=0, concat_axis=0, tiled=True)  35.2 us
    all_to_all x1, waiting for transfers between devices, local(): lax.all_to_all(grad_rows, 'expert', split_axis=0, concat_axis=0, tiled=True)  34.4 us
    all_to_all x1, starting transfers between devices, local(): lax.all_to_all(c_slab, 'expert', split_axis=0, concat_axis=0, tiled=True)  6.65 us
    all_to_all x1, starting transfers between devices, local(): lax.all_to_all(grad_rows, 'expert', split_axis=0, concat_axis=0, tiled=True)  5.63 us
    dot_general x1, matrix products, local(): lax.dot_general(hidden, c_rows, (((0,), (0,)), ((), ())), preferred_eleme...  5.45 us
  transfers between devices with their start and end apart: 7, of which 6 were waited for; matrix products, arithmetic and copies ran while one was open for 11% of the time, Pallas kernels for 0%

profile of v1, /device:TPU:11, one launch (start us, length us, event | category | flops | bytes accessed | tf_op | source)
XLA Modules:
  0.0 262.5 jit_solution(12682456211212196916)
XLA Ops:
  0.6 0.0 copy-start
  0.6 0.8 fusion.36
  1.4 0.1 fusion.31
  1.6 0.7 select_reduce_fusion.1
  2.3 0.1 select_reduce_fusion
  2.4 0.1 mul.46
  2.5 0.1 eq.46
  2.6 0.1 bitcast_compare_fusion
  2.7 0.0 copy-done
  2.8 1.9 multiply_convert_fusion
  4.7 0.0 copy-start.7
  4.7 6.6 %all-to-all-start.2 = ((bf16[16,32,1792]{2,1,0:T(8,128)(2,1)}), bf16[16,32,1792]{2,1,0:T(8,128)(2,1)S(1)}, u32[]{:S(2)}, u32[]{:S(2)}) async-start(bf16[16,32,1792]{2,1,0:T(8,128)(2,1)} %bitcast.8), calls=%async_computation.2 | async-start | bytes 3670016 | tf_op jit(solution)/shard_map/all_to_all | solution.py:58
  11.3 0.0 copy-done.7
  11.3 1.9 convolution_convert_fusion.1
  13.2 39.9 %all-to-all-done.2 = bf16[16,32,1792]{2,1,0:T(8,128)(2,1)S(1)} async-done(((bf16[16,32,1792]{2,1,0:T(8,128)(2,1)}), bf16[16,32,1792]{2,1,0:T(8,128)(2,1)S(1)}, u32[]{:S(2)}, u32[]{:S(2)}) %all-to-all-start.2) | async-done | bytes 1835040 | tf_op jit(solution)/shard_map/all_to_all | solution.py:58
  53.1 0.0 copy-start.1
  53.1 4.8 %all-to-all-start = ((bf16[16,32,1792]{2,1,0:T(8,128)(2,1)}), bf16[16,32,1792]{2,1,0:T(8,128)(2,1)}, u32[]{:S(2)}, u32[]{:S(2)}) async-start(bf16[16,32,1792]{2,1,0:T(8,128)(2,1)} %bitcast.1), calls=%async_computation | async-start | bytes 3670016 | tf_op jit(solution)/shard_map/all_to_all | solution.py:43
  57.9 4.1 %fusion.28 = bf16[512,1024]{1,0:T(8,128)(2,1)S(1)} fusion(bf16[512,1792]{1,0:T(8,128)(2,1)S(1)} %bitcast.55, bf16[1,1024,1792]{2,1,0:T(8,128)(2,1)} %param.12), kind=kOutput, calls=%fused_computation.34 | convolution fusion | flops 1879572480 | bytes 6553600 | tf_op jit(solution)/shard_map/dot_general | solution.py:60
  62.0 0.0 copy-done.1
  62.0 1.3 collective-permute-start.2
  63.3 36.5 %all-to-all-done = bf16[16,32,1792]{2,1,0:T(8,128)(2,1)} async-done(((bf16[16,32,1792]{2,1,0:T(8,128)(2,1)}), bf16[16,32,1792]{2,1,0:T(8,128)(2,1)}, u32[]{:S(2)}, u32[]{:S(2)}) %all-to-all-start) | async-done | bytes 1835040 | tf_op jit(solution)/shard_map/all_to_all | solution.py:43
  99.8 0.0 copy-start.9
  99.8 4.8 %fusion.22 = bf16[512,1024]{1,0:T(8,128)(2,1)S(1)} fusion(bf16[512,1792]{1,0:T(8,128)(2,1)} %bitcast.2, bf16[1,1792,1024]{2,1,0:T(8,128)(2,1)} %param.10), kind=kOutput, calls=%fused_computation.32 | convolution fusion | flops 1879572480 | bytes 6553600 | tf_op jit(solution)/shard_map/dot_general | solution.py:45
  104.6 0.0 copy-done.9
  104.6 0.0 copy-start.8
  104.6 3.7 %fusion.25 = bf16[512,1024]{1,0:T(8,128)(2,1)S(1)} fusion(bf16[512,1792]{1,0:T(8,128)(2,1)} %bitcast.2, bf16[1,1792,1024]{2,1,0:T(8,128)(2,1)S(1)} %copy-done.9), kind=kOutput, calls=%fused_computation.33 | convolution fusion | flops 1879572480 | bytes 6553600 | tf_op jit(solution)/shard_map/dot_general | solution.py:46
  108.4 0.0 copy-start.2
  108.4 1.3 collective-permute-start.1
  109.7 0.2 collective-permute-start
  109.9 0.0 collective-permute-done.2
  109.9 23.1 %collective-permute-done.1 = bf16[512,1024]{1,0:T(8,128)(2,1)S(1)} collective-permute-done((bf16[512,1024]{1,0:T(8,128)(2,1)S(1)}, bf16[512,1024]{1,0:T(8,128)(2,1)S(1)}, u32[]{:S(2)}, u32[]{:S(2)}) %collective-permute-start.1) | collective-permute-done | bytes 1048608 | tf_op jit(solution)/shard_map/ppermute | solution.py:12
  133.1 0.0 copy-start.3
  133.1 22.5 %collective-permute-done = bf16[512,1024]{1,0:T(8,128)(2,1)S(1)} collective-permute-done((bf16[512,1024]{1,0:T(8,128)(2,1)S(1)}, bf16[512,1024]{1,0:T(8,128)(2,1)S(1)}, u32[]{:S(2)}, u32[]{:S(2)}) %collective-permute-start) | collective-permute-done | bytes 1048608 | tf_op jit(solution)/shard_map/ppermute | solution.py:12
  155.5 0.0 copy-done.2
  155.5 0.0 copy-done.3
  155.5 0.0 copy-done.8
  155.5 0.0 copy-start.4
  155.5 4.8 %fusion.8 = f32[512,1792]{1,0:T(8,128)S(1)} fusion(bf16[1,1792,1024]{2,1,0:T(8,128)(2,1)S(1)} %copy-done.8, bf16[512,1024]{1,0:T(8,128)(2,1)S(1)} %collective-permute-done, bf16[512,1024]{1,0:T(8,128)(2,1)S(1)} %fusion.22, bf16[512,1024]{1,0:T(8,128)(2,1)S(1)} %collective-permute-done.1, bf16[512,1024]{1,0:T(8,128)(2,1)S(1)} %fusion.25, ...), kind=kOutput, calls=%fused_computation.9 | convolution fusion | flops 1889009664 | bytes 13631488 | tf_op jit(solution)/shard_map/dot_general | solution.py:65
  160.3 0.0 copy-done.4
  160.4 5.2 %add_convert_fusion = bf16[512,1792]{1,0:T(8,128)(2,1)} fusion(f32[512,1792]{1,0:T(8,128)S(1)} %fusion.8, bf16[1,1792,1024]{2,1,0:T(8,128)(2,1)S(1)} %copy-done.9, bf16[512,1024]{1,0:T(8,128)(2,1)} %collective-permute-done.2, bf16[512,1024]{1,0:T(8,128)(2,1)S(1)} %fusion.28, bf16[512,1024]{1,0:T(8,128)(2,1)S(1)} %collective-permute-done, ...), kind=kOutput, calls=%fused_computation.13 | convolution fusion | flops 1887174656 | bytes 13369344 | tf_op jit(solution)/shard_map/dot_general | solution.py:66
  165.5 5.6 %all-to-all-start.3 = ((bf16[16,32,1792]{2,1,0:T(8,128)(2,1)}), bf16[16,32,1792]{2,1,0:T(8,128)(2,1)S(1)}, u32[]{:S(2)}, u32[]{:S(2)}) async-start(bf16[16,32,1792]{2,1,0:T(8,128)(2,1)} %bitcast.58), calls=%async_computation.3 | async-start | bytes 3670016 | tf_op jit(solution)/shard_map/all_to_all | solution.py:74
  171.2 0.0 copy-start.10
  171.2 3.0 %multiply_convert_fusion.4 = bf16[512,1024]{1,0:T(8,128)(2,1)S(1)} fusion(bf16[512,1024]{1,0:T(8,128)(2,1)} %copy-done.3, bf16[512,1024]{1,0:T(8,128)(2,1)} %copy-done.2, bf16[512,1024]{1,0:T(8,128)(2,1)} %copy-done.4, bf16[512,1024]{1,0:T(8,128)(2,1)S(1)} %fusion.22), kind=kLoop, calls=%fused_computation.26 | loop fusion | flops 6291456 | bytes 5242880 | tf_op jit(solution)/shard_map/convert_element_type | solution.py:49
  174.2 0.0 copy-start.5
  174.2 1.0 copy-done.5
  175.2 0.0 copy-done.10
  175.2 3.3 %fusion.15 = bf16[512,1792]{1,0:T(8,128)(2,1)} fusion(bf16[512,1024]{1,0:T(8,128)(2,1)S(1)} %multiply_convert_fusion.4, bf16[1,1024,1792]{2,1,0:T(8,128)(2,1)S(1)} %copy-done.10), kind=kOutput, calls=%fused_computation.17 | convolution fusion | flops 1879965696 | bytes 6553600 | tf_op jit(solution)/shard_map/dot_general | solution.py:50
  178.6 0.0 copy-start.6
  178.6 34.4 %all-to-all-done.3 = bf16[16,32,1792]{2,1,0:T(8,128)(2,1)S(1)} async-done(((bf16[16,32,1792]{2,1,0:T(8,128)(2,1)}), bf16[16,32,1792]{2,1,0:T(8,128)(2,1)S(1)}, u32[]{:S(2)}, u32[]{:S(2)}) %all-to-all-start.3) | async-done | bytes 1835040 | tf_op jit(solution)/shard_map/all_to_all | solution.py:74
  213.0 4.8 %all-to-all-start.1 = ((bf16[16,32,1792]{2,1,0:T(8,128)(2,1)}), bf16[16,32,1792]{2,1,0:T(8,128)(2,1)}, u32[]{:S(2)}, u32[]{:S(2)}) async-start(bf16[16,32,1792]{2,1,0:T(8,128)(2,1)} %bitcast.57), calls=%async_computation.1 | async-start | bytes 3670016 | tf_op jit(solution)/shard_map/all_to_all | solution.py:57
  217.8 0.0 copy-done.6
  217.8 5.5 %fusion.12 = bf16[1,1024,1792]{2,1,0:T(8,128)(2,1)} fusion(bf16[512,1024]{1,0:T(8,128)(2,1)S(1)} %copy-done.6, bf16[512,1792]{1,0:T(8,128)(2,1)} %bitcast.56), kind=kOutput, calls=%fused_computation.16 | convolution fusion | flops 1880883200 | bytes 6553600 | tf_op jit(solution)/shard_map/dot_general | solution.py:70
  223.2 1.2 fusion.19
  224.4 35.2 %all-to-all-done.1 = bf16[16,32,1792]{2,1,0:T(8,128)(2,1)} async-done(((bf16[16,32,1792]{2,1,0:T(8,128)(2,1)}), bf16[16,32,1792]{2,1,0:T(8,128)(2,1)}, u32[]{:S(2)}, u32[]{:S(2)}) %all-to-all-start.1) | async-done | bytes 1835040 | tf_op jit(solution)/shard_map/all_to_all | solution.py:57
  259.7 2.8 %fusion.18 = bf16[128,1792]{1,0:T(8,128)(2,1)} fusion(bf16[16,32,1792]{2,1,0:T(8,128)(2,1)} %all-to-all-done.1, f32[16,32]{1,0:T(8,128)S(1)} %select_reduce_fusion, s32[16,128]{1,0:T(8,128)S(1)} %fusion.31), kind=kOutput, calls=%fused_computation.21 | convolution fusion | flops 237928448 | bytes 2304000 | tf_op jit(solution)/shard_map/dot_general | solution.py:76
  (1 shorter events, 0.0 us)
Async XLA Ops:
  0.6 2.1 copy-start
  4.7 6.7 %copy-start.7 = (bf16[128,1792]{1,0:T(8,128)(2,1)S(1)}, bf16[128,1792]{1,0:T(8,128)(2,1)}, u32[]{:S(2)}) copy-start(bf16[128,1792]{1,0:T(8,128)(2,1)} %param.7) | copy-start | bytes 1376260
  4.7 48.4 %all-to-all-start.2 = ((bf16[16,32,1792]{2,1,0:T(8,128)(2,1)}), bf16[16,32,1792]{2,1,0:T(8,128)(2,1)S(1)}, u32[]{:S(2)}, u32[]{:S(2)}) async-start(bf16[16,32,1792]{2,1,0:T(8,128)(2,1)} %bitcast.8), calls=%async_computation.2 | async-start | bytes 3670016 | tf_op jit(solution)/shard_map/all_to_all | solution.py:58
  53.1 8.9 %copy-start.1 = (bf16[16,32,1792]{2,1,0:T(8,128)(2,1)}, bf16[16,32,1792]{2,1,0:T(8,128)(2,1)S(1)}, u32[]{:S(2)}) copy-start(bf16[16,32,1792]{2,1,0:T(8,128)(2,1)S(1)} %all-to-all-done.2) | copy-start | bytes 5505028
  53.1 46.7 %all-to-all-start = ((bf16[16,32,1792]{2,1,0:T(8,128)(2,1)}), bf16[16,32,1792]{2,1,0:T(8,128)(2,1)}, u32[]{:S(2)}, u32[]{:S(2)}) async-start(bf16[16,32,1792]{2,1,0:T(8,128)(2,1)} %bitcast.1), calls=%async_computation | async-start | bytes 3670016 | tf_op jit(solution)/shard_map/all_to_all | solution.py:43
  62.0 47.9 %collective-permute-start.2 = (bf16[512,1024]{1,0:T(8,128)(2,1)S(1)}, bf16[512,1024]{1,0:T(8,128)(2,1)}, u32[]{:S(2)}, u32[]{:S(2)}) collective-permute-start(bf16[512,1024]{1,0:T(8,128)(2,1)S(1)} %fusion.28), channel_id=1, source_target_pairs={{0,16},{16,0},{1,17},{17,1},{2,18},{18,2},{3,19},{19,3},{4,20},{20... | collective-permute-start | bytes 3145736 | tf_op jit(solution)/shard_map/ppermute | solution.py:12
  99.8 4.8 %copy-start.9 = (bf16[1,1792,1024]{2,1,0:T(8,128)(2,1)S(1)}, bf16[1,1792,1024]{2,1,0:T(8,128)(2,1)}, u32[]{:S(2)}) copy-start(bf16[1,1792,1024]{2,1,0:T(8,128)(2,1)} %param.11) | copy-start | bytes 11010052
  104.6 50.9 %copy-start.8 = (bf16[1,1792,1024]{2,1,0:T(8,128)(2,1)S(1)}, bf16[1,1792,1024]{2,1,0:T(8,128)(2,1)}, u32[]{:S(2)}) copy-start(bf16[1,1792,1024]{2,1,0:T(8,128)(2,1)} %param.10) | copy-start | bytes 11010052
  108.4 47.2 %copy-start.2 = (bf16[512,1024]{1,0:T(8,128)(2,1)}, bf16[512,1024]{1,0:T(8,128)(2,1)S(1)}, u32[]{:S(2)}) copy-start(bf16[512,1024]{1,0:T(8,128)(2,1)S(1)} %fusion.25) | copy-start | bytes 3145732
  108.4 24.7 %collective-permute-start.1 = (bf16[512,1024]{1,0:T(8,128)(2,1)S(1)}, bf16[512,1024]{1,0:T(8,128)(2,1)S(1)}, u32[]{:S(2)}, u32[]{:S(2)}) collective-permute-start(bf16[512,1024]{1,0:T(8,128)(2,1)S(1)} %fusion.25), channel_id=1, source_target_pairs={{0,16},{16,0},{1,17},{17,1},{2,18},{18,2},{3,19},{19,3},{4,20},{20... | collective-permute-start | bytes 3145736 | tf_op jit(solution)/shard_map/ppermute | solution.py:12
  109.7 45.8 %collective-permute-start = (bf16[512,1024]{1,0:T(8,128)(2,1)S(1)}, bf16[512,1024]{1,0:T(8,128)(2,1)S(1)}, u32[]{:S(2)}, u32[]{:S(2)}) collective-permute-start(bf16[512,1024]{1,0:T(8,128)(2,1)S(1)} %fusion.22), channel_id=1, source_target_pairs={{0,16},{16,0},{1,17},{17,1},{2,18},{18,2},{3,19},{19,3},{4,20},{20... | collective-permute-start | bytes 3145736 | tf_op jit(solution)/shard_map/ppermute | solution.py:12
  133.1 22.5 %copy-start.3 = (bf16[512,1024]{1,0:T(8,128)(2,1)}, bf16[512,1024]{1,0:T(8,128)(2,1)S(1)}, u32[]{:S(2)}) copy-start(bf16[512,1024]{1,0:T(8,128)(2,1)S(1)} %collective-permute-done.1) | copy-start | bytes 3145732
  155.5 4.8 %copy-start.4 = (bf16[512,1024]{1,0:T(8,128)(2,1)}, bf16[512,1024]{1,0:T(8,128)(2,1)S(1)}, u32[]{:S(2)}) copy-start(bf16[512,1024]{1,0:T(8,128)(2,1)S(1)} %collective-permute-done) | copy-start | bytes 3145732
  165.5 47.4 %all-to-all-start.3 = ((bf16[16,32,1792]{2,1,0:T(8,128)(2,1)}), bf16[16,32,1792]{2,1,0:T(8,128)(2,1)S(1)}, u32[]{:S(2)}, u32[]{:S(2)}) async-start(bf16[16,32,1792]{2,1,0:T(8,128)(2,1)} %bitcast.58), calls=%async_computation.3 | async-start | bytes 3670016 | tf_op jit(solution)/shard_map/all_to_all | solution.py:74
  171.2 4.0 %copy-start.10 = (bf16[1,1024,1792]{2,1,0:T(8,128)(2,1)S(1)}, bf16[1,1024,1792]{2,1,0:T(8,128)(2,1)}, u32[]{:S(2)}) copy-start(bf16[1,1024,1792]{2,1,0:T(8,128)(2,1)} %param.12) | copy-start | bytes 11010052
  174.2 1.0 copy-start.5
  178.6 39.2 %copy-start.6 = (bf16[512,1024]{1,0:T(8,128)(2,1)S(1)}, bf16[512,1024]{1,0:T(8,128)(2,1)}, u32[]{:S(2)}) copy-start(bf16[512,1024]{1,0:T(8,128)(2,1)} %copy-done.5) | copy-start | bytes 3145732
  213.0 46.7 %all-to-all-start.1 = ((bf16[16,32,1792]{2,1,0:T(8,128)(2,1)}), bf16[16,32,1792]{2,1,0:T(8,128)(2,1)}, u32[]{:S(2)}, u32[]{:S(2)}) async-start(bf16[16,32,1792]{2,1,0:T(8,128)(2,1)} %bitcast.57), calls=%async_computation.1 | async-start | bytes 3670016 | tf_op jit(solution)/shard_map/all_to_all | solution.py:57
